TPU v7x, 128 devices: a whole 4x4x4 slice. The times are simulated.
128 devices in a mesh: sub: 8 (over z, core), row: 4 (over x), col: 4 (over y).
Axes of the slice: x: 4, y: 4, z: 4, core: 2. Of those that a mesh axis runs over, the one named last changes fastest.
Arguments:
- front: float32 [4, 32, 128, 32, 4, 128], P(None, ('sub', 'row'), None, None, 'col'), may hold values from -2.4 to 7.5, as said below
- child_tiles: bfloat16 [16384, 128, 128], P(('sub', 'row', 'col')), may hold values from -2.390625 to 2.390625
- tile_owner: int32 [16384, 1], P(('sub', 'row', 'col')), may hold values from 0 to 127; in each aligned block of 128 rows (0 to 127, 128 to 255, ...) at most 2 rows name the same one
- tile_slot: int32 [16384], P(('sub', 'row', 'col')), may hold values from 2 to 127
Outputs:
- updated: float32 [4, 32, 128, 32, 4, 128], P(None, ('sub', 'row'), None, None, 'col')
- panel: bfloat16 [4, 32, 128, 2, 4, 128], P(None, ('sub', 'row'), None, None, 'col')
Inputs may be any that keep to these rules, and one draw needn't show every extreme that they name: The leading 1024 x 1024 block of front, made symmetric from its lower triangle, is positive definite. `tile_owner`: at most 2 of the tiles of one device go to one owner.
All inputs are finite; a program needn't handle non-finite values.
Results may differ from a plain program's by a relative error of at most 0.0038.
Values may be sent and summed in bfloat16 or wider, within the bound.
A program may use at most 128 MiB of HBM per device.

v0:
```python
import jax
import jax.numpy as jnp
from jax import lax
from jax.sharding import PartitionSpec as P

NB = 1024


def broadcast(block, axis, source):
    block = jnp.where(lax.axis_index(axis) == source, block, jnp.zeros_like(block))
    return lax.psum(block, axis)


def local(front, child_tiles, tile_owner, tile_slot):
    row_tiles, _, tile_size, col_tiles, _, _ = front.shape
    sub_count = lax.axis_size("sub")
    row_count = lax.axis_size("row")
    col_count = lax.axis_size("col")
    dev_count = sub_count * row_count * col_count
    tile_count = child_tiles.shape[0]
    capacity = max(2, 2 * tile_count // dev_count)
    panel_tiles = NB // tile_size
    per_col = panel_tiles // col_count
    height = row_tiles * tile_size
    local_front = front.reshape(row_tiles, tile_size, col_tiles, tile_size)
    owners = tile_owner[:, 0]
    matches = (owners[:, None] == jnp.arange(dev_count, dtype=jnp.int32)[None, :]).astype(jnp.int32)
    before = jnp.cumsum(matches, 0) - matches
    placed = jnp.sum(before * matches, 1)
    outgoing = (
        jnp.zeros((dev_count, capacity, tile_size, tile_size), jnp.bfloat16)
        .at[owners, placed]
        .set(child_tiles)
    )
    targets = jnp.full((dev_count, capacity), -1, jnp.int32).at[owners, placed].set(tile_slot)
    arrived, landing = (
        lax.all_to_all(outgoing, ("sub", "row", "col"), split_axis=0, concat_axis=0, tiled=True),
        lax.all_to_all(targets, ("sub", "row", "col"), split_axis=0, concat_axis=0, tiled=True),
    )
    arrived = arrived.reshape(dev_count * capacity, tile_size, tile_size)
    landing = landing.reshape(dev_count * capacity)
    selector = (
        landing[:, None] == jnp.arange(row_tiles * col_tiles, dtype=jnp.int32)[None, :]
    ).astype(jnp.bfloat16)
    selector = selector.reshape(dev_count * capacity, row_tiles, col_tiles)
    assembled = local_front + jnp.einsum(
        "kqs,kab->qasb", selector, arrived, preferred_element_type=jnp.float32
    )
    sub_index = lax.axis_index("sub")
    row_index = lax.axis_index("row")
    col_index = lax.axis_index("col")
    group_id = sub_index * row_count + row_index
    corner = assembled[0, :, :per_col, :]
    beside_all = lax.all_gather(corner, ("row", "col"), axis=0, tiled=True)
    beside_all = beside_all.reshape(row_count, col_count, tile_size, per_col, tile_size)
    beside_all = beside_all.transpose(0, 2, 3, 1, 4).reshape(row_count * tile_size, NB)
    blocks = []
    for owner_sub in range(panel_tiles // row_count):
        blocks.append(broadcast(beside_all, "sub", owner_sub))
    pivot = jnp.concatenate(blocks, 0)
    symmetric = jnp.tril(pivot) + jnp.tril(pivot, -1).T
    factor = jnp.linalg.cholesky(symmetric)
    panel_cols = assembled[:, :, :per_col, :].reshape(height, per_col, 1, tile_size)
    widened = lax.all_gather(panel_cols, "col", axis=2, tiled=True).reshape(height, NB)
    solved = jax.scipy.linalg.solve_triangular(factor, widened.T, lower=True).T.astype(jnp.bfloat16)
    leading = lax.dynamic_slice_in_dim(
        factor, jnp.minimum(group_id, panel_tiles - 1) * tile_size, tile_size, 0
    ).astype(jnp.bfloat16)
    upper = jnp.where(group_id < panel_tiles, leading, solved[:tile_size])
    panel_rows = jnp.concatenate([upper, solved[tile_size:]], 0)
    panel_out = lax.dynamic_index_in_dim(
        panel_rows.reshape(row_tiles, tile_size, per_col, col_count, tile_size),
        col_index,
        3,
        keepdims=True,
    )
    panel_out = panel_out.reshape(row_tiles, 1, tile_size, per_col, 1, tile_size)
    across = broadcast(panel_rows, "row", col_index)
    update = jnp.einsum(
        "rk,nqbk->rqnb",
        panel_rows,
        lax.all_gather(across.reshape(1, row_tiles, tile_size, NB), "sub", axis=0, tiled=True),
        preferred_element_type=jnp.float32,
    )
    update = update.reshape(row_tiles, tile_size, col_tiles, tile_size)
    row_tile = jnp.arange(row_tiles, dtype=jnp.int32) * (row_count * sub_count) + group_id
    col_tile = jnp.arange(col_tiles, dtype=jnp.int32) * col_count + col_index
    trailing_mask = (row_tile >= panel_tiles)[:, None, None, None] & (col_tile >= panel_tiles)[
        None, None, :, None
    ]
    result = jnp.where(trailing_mask, assembled - update, assembled)
    return (result.reshape(front.shape), panel_out)


def solution(mesh):
    return jax.shard_map(
        local,
        mesh=mesh,
        in_specs=(
            P(None, ("sub", "row"), None, None, "col", None),
            P(("sub", "row", "col"), None, None),
            P(("sub", "row", "col"), None),
            P(("sub", "row", "col")),
        ),
        out_specs=(
            P(None, ("sub", "row"), None, None, "col", None),
            P(None, ("sub", "row"), None, None, "col", None),
        ),
        check_vma=False,
    )
```

profile of v0, /device:TPU:1, one launch (start us, length us, event | category | flops | bytes accessed | tf_op | source)
XLA Modules:
  0.0 870.7 jit_solution(1453275617700814061)
XLA Ops:
  9.6 11.0 %scatter_fusion.1 = s32[128,2]{0,1:T(2,128)S(1)} fusion(s32[128,2]{0,1:T(2,128)S(1)} %broadcast_in_dim.35, s32[128]{0:T(128)S(1)} %fusion.70, s32[128]{0:T(128)} %param.7), kind=kCustom, calls=%fused_computation.1 | custom fusion | bytes 2560 | tf_op jit(solution)/shard_map/scatter | solution.py:35
  21.3 11.5 %all-to-all-start.1 = ((s32[128,1,2]{2,1,0:T(1,128)}), s32[128,1,2]{2,1,0:T(1,128)S(1)}, u32[]{:S(2)}, u32[]{:S(2)}) async-start(s32[128,1,2]{2,1,0:T(1,128)} %copy.65), calls=%async_computation.1 | async-start | bytes 131072 | tf_op jit(solution)/shard_map/all_to_all | solution.py:38
  32.8 5.5 broadcast_in_dim.34
  38.3 20.7 %scatter_fusion = bf16[128,2,128,128]{3,2,1,0:T(8,128)(2,1)} fusion(bf16[128,2,128,128]{3,2,1,0:T(8,128)(2,1)} %broadcast_in_dim.34, s32[128]{0:T(128)S(1)} %fusion.70, bf16[128,128,128]{2,1,0:T(8,128)(2,1)} %param.5), kind=kCustom, calls=%fused_computation | custom fusion | bytes 12583936 | tf_op jit(solution)/shard_map/scatter | solution.py:33
  59.1 10.2 %all-to-all-start = ((bf16[128,2,128,128]{3,2,1,0:T(8,128)(2,1)}), bf16[128,2,128,128]{3,2,1,0:T(8,128)(2,1)}, u32[]{:S(2)}, u32[]{:S(2)}) async-start(bf16[128,2,128,128]{3,2,1,0:T(8,128)(2,1)} %scatter_fusion), calls=%async_computation | async-start | bytes 16777216 | tf_op jit(solution)/shard_map/all_to_all | solution.py:37
  70.8 99.1 %all-to-all-done = bf16[128,2,128,128]{3,2,1,0:T(8,128)(2,1)} async-done(((bf16[128,2,128,128]{3,2,1,0:T(8,128)(2,1)}), bf16[128,2,128,128]{3,2,1,0:T(8,128)(2,1)}, u32[]{:S(2)}, u32[]{:S(2)}) %all-to-all-start) | async-done | bytes 8388640 | tf_op jit(solution)/shard_map/all_to_all | solution.py:37
  169.9 12.2 %copy.64 = bf16[128,2,128,128]{3,1,0,2:T(2,128)(2,1)S(1)} copy(bf16[128,2,128,128]{3,2,1,0:T(8,128)(2,1)} %all-to-all-done) | data formatting | bytes 16777216 | tf_op jit(solution)/shard_map/all_to_all | solution.py:37
  182.1 5.1 bitcast_add_fusion
  187.3 3.4 copy-done
  194.4 40.8 %all-gather.9.cloned.1.call-done = f32[1,2048,2,128]{3,2,0,1:T(2,128)} async-done(((f32[1,128,2,128]{3,2,0,1:T(2,128)}), f32[1,2048,2,128]{3,2,0,1:T(2,128)}) %all-gather.9.cloned.1.call-update) | async-done | bytes 2097168 | tf_op jit(solution)/shard_map/all_gather | solution.py:54
  235.2 2.7 broadcast_select_fusion
  237.9 2.7 copy.94
  240.6 3.1 select_n.100
  243.7 2.7 copy.95
  246.4 3.2 select_n.95
  249.6 18.8 %all-gather.5.cloned.1.call-done = f32[512,2,4,128]{3,0,1,2:T(8,128)} async-done(((f32[512,2,1,128]{3,0,1,2:T(8,128)}), f32[512,2,4,128]{3,0,1,2:T(8,128)}) %all-gather.5.cloned.1.call-update) | async-done | bytes 2097168 | tf_op jit(solution)/shard_map/all_gather | solution.py:64
  270.4 71.8 %all-reduce.7.cloned.1.call-done = (f32[512,1024]{1,0:T(8,128)}, f32[512,1024]{1,0:T(8,128)}) async-done(((f32[512,1024]{1,0:T(8,128)}, f32[512,1024]{1,0:T(8,128)}), (f32[512,1024]{1,0:T(8,128)}, f32[512,1024]{1,0:T(8,128)})) %all-reduce.7.cloned.1.call-update) | async-done | bytes 4194320 | tf_op jit(solution)/shard_map/psum | solution.py:11
  346.6 2.4 fusion.3
  349.1 5.3 copy.68
  354.4 5.9 bitcast_add_fusion.2
  360.3 5.5 copy.69
  365.9 4.4 fusion.1
  372.2 11.7 %cholesky.222 = f32[128,128]{1,0:T(8,128)S(1)} custom-call(f32[128,128]{1,0:T(8,128)S(1)} %cholesky.577), custom_call_target="Cholesky" | custom-call | tf_op jit(solution)/shard_map/jit(cholesky)/cholesky | solution.py:62
  384.0 2.5 cholesky.254
  386.5 9.8 %custom-call.63 = f32[1,128,128]{1,2,0:T(8,128)S(1)} custom-call(f32[1,128,128]{2,1,0:T(8,128)S(1)} %get-tuple-element.74), custom_call_target="InvertDiagBlocksLowerTriangular" | custom-call | tf_op jit(solution)/shard_map/jit(cholesky)/cholesky | solution.py:62
  396.3 2.4 constant_dynamic-update-slice_fusion.27
  400.2 12.1 %cholesky.243 = f32[128,128]{1,0:T(8,128)S(1)} custom-call(f32[128,128]{1,0:T(8,128)S(1)} %cholesky.581), custom_call_target="Cholesky" | custom-call | tf_op jit(solution)/shard_map/jit(cholesky)/cholesky | solution.py:62
  413.0 9.8 %custom-call.64 = f32[1,128,128]{1,2,0:T(8,128)S(1)} custom-call(f32[1,128,128]{2,1,0:T(8,128)S(1)} %get-tuple-element.71), custom_call_target="InvertDiagBlocksLowerTriangular" | custom-call | tf_op jit(solution)/shard_map/jit(cholesky)/cholesky | solution.py:62
  426.1 11.7 %cholesky.466 = f32[128,128]{1,0:T(8,128)S(1)} custom-call(f32[128,128]{1,0:T(8,128)S(1)} %cholesky.586), custom_call_target="Cholesky" | custom-call | tf_op jit(solution)/shard_map/jit(cholesky)/cholesky | solution.py:62
  439.1 9.8 %custom-call.65 = f32[1,128,128]{1,2,0:T(8,128)S(1)} custom-call(f32[1,128,128]{2,1,0:T(8,128)S(1)} %get-tuple-element.68), custom_call_target="InvertDiagBlocksLowerTriangular" | custom-call | tf_op jit(solution)/shard_map/jit(cholesky)/cholesky | solution.py:62
  450.1 2.3 convolution_subtract_fusion.2
  452.4 11.8 %cholesky.485 = f32[128,128]{1,0:T(8,128)S(1)} custom-call(f32[128,128]{1,0:T(8,128)S(1)} %cholesky.591), custom_call_target="Cholesky" | custom-call | tf_op jit(solution)/shard_map/jit(cholesky)/cholesky | solution.py:62
  465.6 9.8 %custom-call.66 = f32[1,128,128]{1,2,0:T(8,128)S(1)} custom-call(f32[1,128,128]{2,1,0:T(8,128)S(1)} %get-tuple-element.65), custom_call_target="InvertDiagBlocksLowerTriangular" | custom-call | tf_op jit(solution)/shard_map/jit(cholesky)/cholesky | solution.py:62
  476.5 2.3 convolution_subtract_fusion.10
  478.8 11.7 %cholesky.504 = f32[128,128]{1,0:T(8,128)S(1)} custom-call(f32[128,128]{1,0:T(8,128)S(1)} %cholesky.596), custom_call_target="Cholesky" | custom-call | tf_op jit(solution)/shard_map/jit(cholesky)/cholesky | solution.py:62
  491.8 10.0 %custom-call.67 = f32[1,128,128]{1,2,0:T(8,128)S(1)} custom-call(f32[1,128,128]{2,1,0:T(8,128)S(1)} %get-tuple-element.62), custom_call_target="InvertDiagBlocksLowerTriangular" | custom-call | tf_op jit(solution)/shard_map/jit(cholesky)/cholesky | solution.py:62
  502.9 2.3 convolution_subtract_fusion.11
  505.2 11.7 %cholesky.524 = f32[128,128]{1,0:T(8,128)S(1)} custom-call(f32[128,128]{1,0:T(8,128)S(1)} %cholesky.601), custom_call_target="Cholesky" | custom-call | tf_op jit(solution)/shard_map/jit(cholesky)/cholesky | solution.py:62
  518.1 9.8 %custom-call.68 = f32[1,128,128]{1,2,0:T(8,128)S(1)} custom-call(f32[1,128,128]{2,1,0:T(8,128)S(1)} %get-tuple-element.59), custom_call_target="InvertDiagBlocksLowerTriangular" | custom-call | tf_op jit(solution)/shard_map/jit(cholesky)/cholesky | solution.py:62
  531.0 12.1 %cholesky.544 = f32[128,128]{1,0:T(8,128)S(1)} custom-call(f32[128,128]{1,0:T(8,128)S(1)} %cholesky.606), custom_call_target="Cholesky" | custom-call | tf_op jit(solution)/shard_map/jit(cholesky)/cholesky | solution.py:62
  544.3 9.8 %custom-call.69 = f32[1,128,128]{1,2,0:T(8,128)S(1)} custom-call(f32[1,128,128]{2,1,0:T(8,128)S(1)} %get-tuple-element.56), custom_call_target="InvertDiagBlocksLowerTriangular" | custom-call | tf_op jit(solution)/shard_map/jit(cholesky)/cholesky | solution.py:62
  556.7 11.7 %cholesky.562 = f32[128,128]{1,0:T(8,128)S(1)} custom-call(f32[128,128]{1,0:T(8,128)S(1)} %convolution_subtract_fusion.13), custom_call_target="Cholesky" | custom-call | tf_op jit(solution)/shard_map/jit(cholesky)/cholesky | solution.py:62
  575.3 5.8 fusion.2
  581.1 27.9 %while.1 = (s32[]{:T(128)}, f32[1024,1024]{1,0:T(8,128)}, s32[8,2]{0,1:T(2,128)S(1)}, f32[8,128,128]{2,1,0:T(8,128)}, s32[]{:T(128)}) while((s32[]{:T(128)}, f32[1024,1024]{1,0:T(8,128)}, s32[8,2]{0,1:T(2,128)S(1)}, f32[8,128,128]{2,1,0:T(8,128)}, s32[]{:T(128)}) %tuple.68), condition=%wide.while_cond, body=%wide.while_body.sunk | while | flops 2 | bytes 132705 | solution.py:65
  581.8 2.8 bitcast_dynamic-update-slice_fusion.2
  585.3 2.8 bitcast_dynamic-update-slice_fusion.2
  588.8 2.8 bitcast_dynamic-update-slice_fusion.2
  592.3 2.8 bitcast_dynamic-update-slice_fusion.2
  595.7 2.8 bitcast_dynamic-update-slice_fusion.2
  599.2 2.8 bitcast_dynamic-update-slice_fusion.2
  602.7 2.8 bitcast_dynamic-update-slice_fusion.2
  606.2 2.8 bitcast_dynamic-update-slice_fusion.2
  609.0 79.6 %custom-call.70 = f32[8,128,128]{1,2,0:T(8,128)S(1)} custom-call(f32[8,128,128]{2,1,0:T(8,128)} %get-tuple-element.9), custom_call_target="InvertDiagBlocksLowerTriangular" | custom-call | tf_op jit(solution)/shard_map/jit(_solve_triangular)/triangular_solve | solution.py:65
  696.8 2.2 constant_dynamic-update-slice_fusion.16
  701.2 2.2 constant_dynamic-update-slice_fusion.15
  703.4 2.3 convolution_subtract_fusion.4
  707.8 2.5 convolution_subtract_fusion.7
  712.3 2.9 convolution_subtract_fusion.3
  719.9 45.9 %all-reduce.5.cloned.1.call-done = bf16[1,4,128,1024]{3,2,1,0:T(8,128)(2,1)} async-done(((bf16[1,4,128,1024]{3,2,1,0:T(8,128)(2,1)}), bf16[1,4,128,1024]{3,2,1,0:T(8,128)(2,1)}) %all-reduce.5.cloned.1.call-update) | async-done | bytes 1048592 | tf_op jit(solution)/shard_map/psum | solution.py:11
  768.5 52.0 %all-gather.7.cloned.1.call-done = bf16[8,4,128,1024]{3,2,1,0:T(8,128)(2,1)} async-done(((bf16[1,4,128,1024]{3,2,1,0:T(8,128)(2,1)}), bf16[8,4,128,1024]{3,2,1,0:T(8,128)(2,1)}) %all-gather.7.cloned.1.call-update) | async-done | bytes 8388624 | tf_op jit(solution)/shard_map/all_gather | solution.py:82
  820.5 10.4 %convolution_bitcast_fusion = f32[512,4,8,128]{0,3,1,2:T(8,128)} fusion(bf16[8,4,128,1024]{3,2,1,0:T(8,128)(2,1)} %all-gather.7.cloned.1.call-done, bf16[384,1024]{1,0:T(8,128)(2,1)S(1)} %slice.280, bf16[128,1024]{1,0:T(8,128)(2,1)S(1)} %fusion.36), kind=kOutput, calls=%fused_computation.15 | convolution fusion | flops 4297064448 | bytes 17825792 | tf_op jit(solution)/shard_map/rk,nqbk->rqnb/dot_general | solution.py:79
  830.8 10.4 %copy.80 = f32[512,4,8,128]{3,2,1,0:T(8,128)} copy(f32[512,4,8,128]{0,3,1,2:T(8,128)} %convolution_bitcast_fusion) | data formatting | bytes 16777216 | tf_op jit(solution)/shard_map/rk,nqbk->rqnb/transpose | solution.py:79
  841.3 11.7 %fusion = f32[4,1,128,32,1,128]{5,3,0,2,4,1:T(8,128)} fusion(f32[4,128,32,128]{3,2,0,1:T(8,128)} %copy-done, f32[4,128,32,128]{3,2,1,0:T(8,128)} %bitcast.154, pred[4,32]{1,0:T(4,128)(4,1)S(1)} %broadcast_and_fusion), kind=kLoop, calls=%fused_computation.5 | loop fusion | flops 4194304 | bytes 25165952 | tf_op jit(solution)/shard_map/reshape | solution.py:92
  853.0 11.0 %copy.83 = f32[4,1,128,32,1,128]{5,4,3,2,1,0:T(1,128)} copy(f32[4,1,128,32,1,128]{5,3,0,2,4,1:T(8,128)} %fusion) | data formatting | bytes 16777216
  (122 shorter events, 66.4 us)
Async XLA Ops:
  21.3 37.7 %all-to-all-start.1 = ((s32[128,1,2]{2,1,0:T(1,128)}), s32[128,1,2]{2,1,0:T(1,128)S(1)}, u32[]{:S(2)}, u32[]{:S(2)}) async-start(s32[128,1,2]{2,1,0:T(1,128)} %copy.65), calls=%async_computation.1 | async-start | bytes 131072 | tf_op jit(solution)/shard_map/all_to_all | solution.py:38
  59.1 110.8 %all-to-all-start = ((bf16[128,2,128,128]{3,2,1,0:T(8,128)(2,1)}), bf16[128,2,128,128]{3,2,1,0:T(8,128)(2,1)}, u32[]{:S(2)}, u32[]{:S(2)}) async-start(bf16[128,2,128,128]{3,2,1,0:T(8,128)(2,1)} %scatter_fusion), calls=%async_computation | async-start | bytes 16777216 | tf_op jit(solution)/shard_map/all_to_all | solution.py:37
  69.3 165.9 %all-gather.9.cloned.1.call-start = ((), (), s32[]{:S(2)}) async-start(), calls=%async_computation.5 | async-start | bytes 2228224 | tf_op jit(solution)/shard_map/all_gather | solution.py:54
  187.2 3.4 copy-start
  191.4 77.1 %all-gather.5.cloned.1.call-start = ((), (), s32[]{:S(2)}) async-start(), calls=%async_computation.2 | async-start | bytes 2621440 | tf_op jit(solution)/shard_map/all_gather | solution.py:64
  194.2 148.1 %all-reduce.7.cloned.1.call-start = ((), (), s32[]{:S(2)}) async-start(), calls=%async_computation.6 | async-start | bytes 8388608 | tf_op jit(solution)/shard_map/psum | solution.py:11
  249.5 516.3 %all-reduce.5.cloned.1.call-start = ((), (), s32[]{:S(2)}) async-start(), calls=%async_computation.3 | async-start | bytes 2097152 | tf_op jit(solution)/shard_map/psum | solution.py:11
  342.2 2.2 copy-start.3
  344.7 1.9 copy-start.1
  370.3 1.9 copy-start.2
  688.6 8.2 copy-start.4
  719.9 100.6 %all-gather.7.cloned.1.call-start = ((), (), s32[]{:S(2)}) async-start(), calls=%async_computation.4 | async-start | bytes 9437184 | tf_op jit(solution)/shard_map/all_gather | solution.py:82
Sparse Core Ops, SparseCore 0:
  191.5 43.6 all-gather.8
  236.9 31.5 all-gather.4
  270.9 71.2 all-reduce.6
  720.0 45.8 all-reduce.4
  767.4 53.0 all-gather.6
where the time goes:
time: 878 us; the launch traced here: 871 us
  waiting for transfers between devices  329 us (37%)
  other arithmetic  291 us (33%)
  local copies, waits for them, and re-layouts  144 us (16%)
  matrix products  66.1 us (8%)
  starting transfers between devices  22.1 us (3%)
  between operations  19.5 us (2%)
    another operation x30, other arithmetic, local(): factor = jnp.linalg.cholesky(symmetric)  172 us
    psum x2, waiting for transfers between devices, broadcast(): return lax.psum(block, axis)  118 us
    all_to_all x1, waiting for transfers between devices, local(): lax.all_to_all(outgoing, ('sub', 'row', 'col'), split_axis=0, concat_axis...  99.1 us
    another operation x3, other arithmetic, local(): jax.scipy.linalg.solve_triangular(factor, widened.T, lower=True)  85.4 us
    all_gather x1, waiting for transfers between devices, local(): lax.all_gather(across.reshape(1, row_tiles, tile_size, NB), 'sub', axis=0...  52 us
    all_gather x1, waiting for transfers between devices, local(): beside_all = lax.all_gather(corner, ('row', 'col'), axis=0, tiled=True)  40.8 us
    another operation x24, local copies, waits for them, and re-layouts  27.9 us
    another operation x15, matrix products, local(): jax.scipy.linalg.solve_triangular(factor, widened.T, lower=True)  27.5 us
  transfers between devices with their start and end apart: 7, of which 6 were waited for; matrix products, arithmetic and copies ran while one was open for 6% of the time, Pallas kernels for 0%

commit v1 on v0

--- a/solution.py
+++ b/solution.py
@@ -79,7 +79,15 @@
     update = jnp.einsum(
         "rk,nqbk->rqnb",
         panel_rows,
-        lax.all_gather(across.reshape(1, row_tiles, tile_size, NB), "sub", axis=0, tiled=True),
+        jnp.concatenate(
+            lax.all_to_all(
+                jnp.stack([across.reshape(1, row_tiles, tile_size, NB)] * lax.axis_size("sub")),
+                "sub",
+                0,
+                0,
+            ),
+            axis=0,
+        ),
         preferred_element_type=jnp.float32,
     )
     update = update.reshape(row_tiles, tile_size, col_tiles, tile_size)

time: 878 us -> 931 us (1.060)
  waiting for transfers between devices: 329 us -> 368 us
    all_to_all x0 -> x1, waiting for transfers between devices: none -> 91.2 us  [local(): lax.all_to_all(jnp.stack([across.reshape(1, row_tiles, tile_size, NB)] *...]
    all_gather x1 -> x0, waiting for transfers between devices: 52 us -> none  [local(): lax.all_gather(across.reshape(1, row_tiles, tile_size, NB), 'sub', axis=0...]
    another operation x24 -> x25, local copies, waits for them, and re-layouts: 27.9 us -> 33.4 us
  transfers between devices with their start and end apart: 7 -> 7, of which waited for: 6 -> 6; matrix products, arithmetic and copies ran while one was open for 6% -> 5% of each run, Pallas kernels for 0% -> 0%
where the time goes in v1:
time: 931 us; the launch traced here: 923 us
  waiting for transfers between devices  368 us (40%)
  other arithmetic  291 us (31%)
  local copies, waits for them, and re-layouts  149 us (16%)
  matrix products  66.1 us (7%)
  starting transfers between devices  29.6 us (3%)
  between operations  19.4 us (2%)
    another operation x30, other arithmetic, local(): factor = jnp.linalg.cholesky(symmetric)  172 us
    psum x2, waiting for transfers between devices, broadcast(): return lax.psum(block, axis)  118 us
    all_to_all x1, waiting for transfers between devices, local(): lax.all_to_all(outgoing, ('sub', 'row', 'col'), split_axis=0, concat_axis...  99.1 us
    all_to_all x1, waiting for transfers between devices, local(): lax.all_to_all(jnp.stack([across.reshape(1, row_tiles, tile_size, NB)] *...  91.2 us
    another operation x3, other arithmetic, local(): jax.scipy.linalg.solve_triangular(factor, widened.T, lower=True)  85.4 us
    all_gather x1, waiting for transfers between devices, local(): beside_all = lax.all_gather(corner, ('row', 'col'), axis=0, tiled=True)  40.8 us
    another operation x24, local copies, waits for them, and re-layouts  27.9 us
    another operation x15, matrix products, local(): jax.scipy.linalg.solve_triangular(factor, widened.T, lower=True)  27.5 us
  transfers between devices with their start and end apart: 7, of which 6 were waited for; matrix products, arithmetic and copies ran while one was open for 5% of the time, Pallas kernels for 0%

profile of v1, /device:TPU:1, one launch (start us, length us, event | category | flops | bytes accessed | tf_op | source)
XLA Modules:
  0.0 922.9 jit_solution(8403412075255145358)
XLA Ops:
  9.6 11.0 %scatter_fusion.1 = s32[128,2]{0,1:T(2,128)S(1)} fusion(s32[128,2]{0,1:T(2,128)S(1)} %broadcast_in_dim.35, s32[128]{0:T(128)S(1)} %fusion.75, s32[128]{0:T(128)} %param.7), kind=kCustom, calls=%fused_computation.1 | custom fusion | bytes 2560 | tf_op jit(solution)/shard_map/scatter | solution.py:35
  21.3 11.5 %all-to-all-start.1 = ((s32[128,1,2]{2,1,0:T(1,128)}), s32[128,1,2]{2,1,0:T(1,128)S(1)}, u32[]{:S(2)}, u32[]{:S(2)}) async-start(s32[128,1,2]{2,1,0:T(1,128)} %copy.65), calls=%async_computation.1 | async-start | bytes 131072 | tf_op jit(solution)/shard_map/all_to_all | solution.py:38
  32.8 5.5 broadcast_in_dim.34
  38.3 20.7 %scatter_fusion = bf16[128,2,128,128]{3,2,1,0:T(8,128)(2,1)} fusion(bf16[128,2,128,128]{3,2,1,0:T(8,128)(2,1)} %broadcast_in_dim.34, s32[128]{0:T(128)S(1)} %fusion.75, bf16[128,128,128]{2,1,0:T(8,128)(2,1)} %param.5), kind=kCustom, calls=%fused_computation | custom fusion | bytes 12583936 | tf_op jit(solution)/shard_map/scatter | solution.py:33
  59.1 10.2 %all-to-all-start = ((bf16[128,2,128,128]{3,2,1,0:T(8,128)(2,1)}), bf16[128,2,128,128]{3,2,1,0:T(8,128)(2,1)}, u32[]{:S(2)}, u32[]{:S(2)}) async-start(bf16[128,2,128,128]{3,2,1,0:T(8,128)(2,1)} %scatter_fusion), calls=%async_computation | async-start | bytes 16777216 | tf_op jit(solution)/shard_map/all_to_all | solution.py:37
  70.8 99.1 %all-to-all-done = bf16[128,2,128,128]{3,2,1,0:T(8,128)(2,1)} async-done(((bf16[128,2,128,128]{3,2,1,0:T(8,128)(2,1)}), bf16[128,2,128,128]{3,2,1,0:T(8,128)(2,1)}, u32[]{:S(2)}, u32[]{:S(2)}) %all-to-all-start) | async-done | bytes 8388640 | tf_op jit(solution)/shard_map/all_to_all | solution.py:37
  169.9 12.2 %copy.64 = bf16[128,2,128,128]{3,1,0,2:T(2,128)(2,1)S(1)} copy(bf16[128,2,128,128]{3,2,1,0:T(8,128)(2,1)} %all-to-all-done) | data formatting | bytes 16777216 | tf_op jit(solution)/shard_map/all_to_all | solution.py:37
  182.1 5.1 bitcast_add_fusion
  187.3 3.4 copy-done
  194.4 40.8 %all-gather.6.cloned.1.call-done = f32[1,2048,2,128]{3,2,0,1:T(2,128)} async-done(((f32[1,128,2,128]{3,2,0,1:T(2,128)}), f32[1,2048,2,128]{3,2,0,1:T(2,128)}) %all-gather.6.cloned.1.call-update) | async-done | bytes 2097168 | tf_op jit(solution)/shard_map/all_gather | solution.py:54
  235.2 2.7 broadcast_select_fusion
  237.9 2.7 copy.94
  240.6 3.1 select_n.100
  243.7 2.7 copy.95
  246.4 3.2 select_n.95
  249.6 18.8 %all-gather.4.cloned.1.call-done = f32[512,2,4,128]{3,0,1,2:T(8,128)} async-done(((f32[512,2,1,128]{3,0,1,2:T(8,128)}), f32[512,2,4,128]{3,0,1,2:T(8,128)}) %all-gather.4.cloned.1.call-update) | async-done | bytes 2097168 | tf_op jit(solution)/shard_map/all_gather | solution.py:64
  270.4 71.8 %all-reduce.7.cloned.1.call-done = (f32[512,1024]{1,0:T(8,128)}, f32[512,1024]{1,0:T(8,128)}) async-done(((f32[512,1024]{1,0:T(8,128)}, f32[512,1024]{1,0:T(8,128)}), (f32[512,1024]{1,0:T(8,128)}, f32[512,1024]{1,0:T(8,128)})) %all-reduce.7.cloned.1.call-update) | async-done | bytes 4194320 | tf_op jit(solution)/shard_map/psum | solution.py:11
  346.6 2.4 fusion.5
  349.1 5.3 copy.68
  354.4 5.9 bitcast_add_fusion.2
  360.3 5.5 copy.69
  365.9 4.4 fusion.3
  372.2 11.7 %cholesky.222 = f32[128,128]{1,0:T(8,128)S(1)} custom-call(f32[128,128]{1,0:T(8,128)S(1)} %cholesky.577), custom_call_target="Cholesky" | custom-call | tf_op jit(solution)/shard_map/jit(cholesky)/cholesky | solution.py:62
  384.0 2.5 cholesky.254
  386.5 9.8 %custom-call.63 = f32[1,128,128]{1,2,0:T(8,128)S(1)} custom-call(f32[1,128,128]{2,1,0:T(8,128)S(1)} %get-tuple-element.74), custom_call_target="InvertDiagBlocksLowerTriangular" | custom-call | tf_op jit(solution)/shard_map/jit(cholesky)/cholesky | solution.py:62
  396.3 2.4 constant_dynamic-update-slice_fusion.27
  400.2 12.1 %cholesky.243 = f32[128,128]{1,0:T(8,128)S(1)} custom-call(f32[128,128]{1,0:T(8,128)S(1)} %cholesky.581), custom_call_target="Cholesky" | custom-call | tf_op jit(solution)/shard_map/jit(cholesky)/cholesky | solution.py:62
  413.0 9.8 %custom-call.64 = f32[1,128,128]{1,2,0:T(8,128)S(1)} custom-call(f32[1,128,128]{2,1,0:T(8,128)S(1)} %get-tuple-element.71), custom_call_target="InvertDiagBlocksLowerTriangular" | custom-call | tf_op jit(solution)/shard_map/jit(cholesky)/cholesky | solution.py:62
  426.1 11.7 %cholesky.466 = f32[128,128]{1,0:T(8,128)S(1)} custom-call(f32[128,128]{1,0:T(8,128)S(1)} %cholesky.586), custom_call_target="Cholesky" | custom-call | tf_op jit(solution)/shard_map/jit(cholesky)/cholesky | solution.py:62
  439.1 9.8 %custom-call.65 = f32[1,128,128]{1,2,0:T(8,128)S(1)} custom-call(f32[1,128,128]{2,1,0:T(8,128)S(1)} %get-tuple-element.68), custom_call_target="InvertDiagBlocksLowerTriangular" | custom-call | tf_op jit(solution)/shard_map/jit(cholesky)/cholesky | solution.py:62
  450.1 2.3 convolution_subtract_fusion.2
  452.4 11.8 %cholesky.485 = f32[128,128]{1,0:T(8,128)S(1)} custom-call(f32[128,128]{1,0:T(8,128)S(1)} %cholesky.591), custom_call_target="Cholesky" | custom-call | tf_op jit(solution)/shard_map/jit(cholesky)/cholesky | solution.py:62
  465.6 9.8 %custom-call.66 = f32[1,128,128]{1,2,0:T(8,128)S(1)} custom-call(f32[1,128,128]{2,1,0:T(8,128)S(1)} %get-tuple-element.65), custom_call_target="InvertDiagBlocksLowerTriangular" | custom-call | tf_op jit(solution)/shard_map/jit(cholesky)/cholesky | solution.py:62
  476.5 2.3 convolution_subtract_fusion.10
  478.8 11.7 %cholesky.504 = f32[128,128]{1,0:T(8,128)S(1)} custom-call(f32[128,128]{1,0:T(8,128)S(1)} %cholesky.596), custom_call_target="Cholesky" | custom-call | tf_op jit(solution)/shard_map/jit(cholesky)/cholesky | solution.py:62
  491.8 10.0 %custom-call.67 = f32[1,128,128]{1,2,0:T(8,128)S(1)} custom-call(f32[1,128,128]{2,1,0:T(8,128)S(1)} %get-tuple-element.62), custom_call_target="InvertDiagBlocksLowerTriangular" | custom-call | tf_op jit(solution)/shard_map/jit(cholesky)/cholesky | solution.py:62
  502.9 2.3 convolution_subtract_fusion.11
  505.2 11.7 %cholesky.524 = f32[128,128]{1,0:T(8,128)S(1)} custom-call(f32[128,128]{1,0:T(8,128)S(1)} %cholesky.601), custom_call_target="Cholesky" | custom-call | tf_op jit(solution)/shard_map/jit(cholesky)/cholesky | solution.py:62
  518.1 9.8 %custom-call.68 = f32[1,128,128]{1,2,0:T(8,128)S(1)} custom-call(f32[1,128,128]{2,1,0:T(8,128)S(1)} %get-tuple-element.59), custom_call_target="InvertDiagBlocksLowerTriangular" | custom-call | tf_op jit(solution)/shard_map/jit(cholesky)/cholesky | solution.py:62
  531.0 12.1 %cholesky.544 = f32[128,128]{1,0:T(8,128)S(1)} custom-call(f32[128,128]{1,0:T(8,128)S(1)} %cholesky.606), custom_call_target="Cholesky" | custom-call | tf_op jit(solution)/shard_map/jit(cholesky)/cholesky | solution.py:62
  544.3 9.8 %custom-call.69 = f32[1,128,128]{1,2,0:T(8,128)S(1)} custom-call(f32[1,128,128]{2,1,0:T(8,128)S(1)} %get-tuple-element.56), custom_call_target="InvertDiagBlocksLowerTriangular" | custom-call | tf_op jit(solution)/shard_map/jit(cholesky)/cholesky | solution.py:62
  556.7 11.7 %cholesky.562 = f32[128,128]{1,0:T(8,128)S(1)} custom-call(f32[128,128]{1,0:T(8,128)S(1)} %convolution_subtract_fusion.13), custom_call_target="Cholesky" | custom-call | tf_op jit(solution)/shard_map/jit(cholesky)/cholesky | solution.py:62
  575.3 5.8 fusion.4
  581.1 27.9 %while.1 = (s32[]{:T(128)}, f32[1024,1024]{1,0:T(8,128)}, s32[8,2]{0,1:T(2,128)S(1)}, f32[8,128,128]{2,1,0:T(8,128)}, s32[]{:T(128)}) while((s32[]{:T(128)}, f32[1024,1024]{1,0:T(8,128)}, s32[8,2]{0,1:T(2,128)S(1)}, f32[8,128,128]{2,1,0:T(8,128)}, s32[]{:T(128)}) %tuple.68), condition=%wide.while_cond, body=%wide.while_body.sunk | while | flops 2 | bytes 132705 | solution.py:65
  581.8 2.8 bitcast_dynamic-update-slice_fusion.2
  585.3 2.8 bitcast_dynamic-update-slice_fusion.2
  588.8 2.8 bitcast_dynamic-update-slice_fusion.2
  592.3 2.8 bitcast_dynamic-update-slice_fusion.2
  595.7 2.8 bitcast_dynamic-update-slice_fusion.2
  599.2 2.8 bitcast_dynamic-update-slice_fusion.2
  602.7 2.8 bitcast_dynamic-update-slice_fusion.2
  606.2 2.8 bitcast_dynamic-update-slice_fusion.2
  609.0 79.6 %custom-call.70 = f32[8,128,128]{1,2,0:T(8,128)S(1)} custom-call(f32[8,128,128]{2,1,0:T(8,128)} %get-tuple-element.9), custom_call_target="InvertDiagBlocksLowerTriangular" | custom-call | tf_op jit(solution)/shard_map/jit(_solve_triangular)/triangular_solve | solution.py:65
  703.4 2.3 convolution_subtract_fusion.4
  707.8 2.5 convolution_subtract_fusion.7
  712.3 2.9 convolution_subtract_fusion.3
  719.9 46.0 %all-reduce.5.cloned.1.call-done = bf16[4,128,1024]{2,1,0:T(8,128)(2,1)} async-done(((bf16[4,128,1024]{2,1,0:T(8,128)(2,1)}), bf16[4,128,1024]{2,1,0:T(8,128)(2,1)}) %all-reduce.5.cloned.1.call-update) | async-done | bytes 1048592 | tf_op jit(solution)/shard_map/psum | solution.py:11
  765.9 5.5 stack.3
  771.4 7.6 all-to-all-start.2
  781.4 91.2 %all-to-all-done.2 = bf16[8,1,4,128,1024]{4,3,2,1,0:T(8,128)(2,1)} async-done(((bf16[8,1,4,128,1024]{4,3,2,1,0:T(8,128)(2,1)}), bf16[8,1,4,128,1024]{4,3,2,1,0:T(8,128)(2,1)}, u32[]{:S(2)}, u32[]{:S(2)}) %all-to-all-start.2) | async-done | bytes 8388640 | tf_op jit(solution)/shard_map/all_to_all | solution.py:83
  872.7 10.4 %fusion.6 = f32[512,4,8,128]{0,3,1,2:T(8,128)} fusion(bf16[8,1,4,128,1024]{4,3,2,1,0:T(8,128)(2,1)} %all-to-all-done.2, bf16[384,1024]{1,0:T(8,128)(2,1)S(1)} %slice.280, bf16[128,1024]{1,0:T(8,128)(2,1)S(1)} %fusion.41), kind=kOutput, calls=%fused_computation.17 | convolution fusion | flops 4297064448 | bytes 17825792 | tf_op jit(solution)/shard_map/rk,nqbk->rqnb/dot_general | solution.py:79
  883.0 10.4 %copy.80 = f32[512,4,8,128]{3,2,1,0:T(8,128)} copy(f32[512,4,8,128]{0,3,1,2:T(8,128)} %fusion.6) | data formatting | bytes 16777216 | tf_op jit(solution)/shard_map/rk,nqbk->rqnb/transpose | solution.py:79
  893.5 11.7 %fusion = f32[4,1,128,32,1,128]{5,3,0,2,4,1:T(8,128)} fusion(f32[4,128,32,128]{3,2,0,1:T(8,128)} %copy-done, f32[4,128,32,128]{3,2,1,0:T(8,128)} %bitcast.158, pred[4,32]{1,0:T(4,128)(4,1)S(1)} %broadcast_and_fusion), kind=kLoop, calls=%fused_computation.5 | loop fusion | flops 4194304 | bytes 25165952 | tf_op jit(solution)/shard_map/reshape | solution.py:100
  905.2 11.0 %copy.83 = f32[4,1,128,32,1,128]{5,4,3,2,1,0:T(1,128)} copy(f32[4,1,128,32,1,128]{5,3,0,2,4,1:T(8,128)} %fusion) | data formatting | bytes 16777216
  (122 shorter events, 70.6 us)
Async XLA Ops:
  21.3 37.7 %all-to-all-start.1 = ((s32[128,1,2]{2,1,0:T(1,128)}), s32[128,1,2]{2,1,0:T(1,128)S(1)}, u32[]{:S(2)}, u32[]{:S(2)}) async-start(s32[128,1,2]{2,1,0:T(1,128)} %copy.65), calls=%async_computation.1 | async-start | bytes 131072 | tf_op jit(solution)/shard_map/all_to_all | solution.py:38
  59.1 110.8 %all-to-all-start = ((bf16[128,2,128,128]{3,2,1,0:T(8,128)(2,1)}), bf16[128,2,128,128]{3,2,1,0:T(8,128)(2,1)}, u32[]{:S(2)}, u32[]{:S(2)}) async-start(bf16[128,2,128,128]{3,2,1,0:T(8,128)(2,1)} %scatter_fusion), calls=%async_computation | async-start | bytes 16777216 | tf_op jit(solution)/shard_map/all_to_all | solution.py:37
  69.3 165.9 %all-gather.6.cloned.1.call-start = ((), (), s32[]{:S(2)}) async-start(), calls=%async_computation.5 | async-start | bytes 2228224 | tf_op jit(solution)/shard_map/all_gather | solution.py:54
  187.2 3.4 copy-start
  191.4 77.1 %all-gather.4.cloned.1.call-start = ((), (), s32[]{:S(2)}) async-start(), calls=%async_computation.3 | async-start | bytes 2621440 | tf_op jit(solution)/shard_map/all_gather | solution.py:64
  194.2 148.1 %all-reduce.7.cloned.1.call-start = ((), (), s32[]{:S(2)}) async-start(), calls=%async_computation.6 | async-start | bytes 8388608 | tf_op jit(solution)/shard_map/psum | solution.py:11
  249.5 516.3 %all-reduce.5.cloned.1.call-start = ((), (), s32[]{:S(2)}) async-start(), calls=%async_computation.4 | async-start | bytes 2097152 | tf_op jit(solution)/shard_map/psum | solution.py:11
  342.2 2.2 copy-start.3
  344.7 1.9 copy-start.1
  370.3 1.9 copy-start.2
  688.6 8.2 copy-start.4
  771.4 101.3 %all-to-all-start.2 = ((bf16[8,1,4,128,1024]{4,3,2,1,0:T(8,128)(2,1)}), bf16[8,1,4,128,1024]{4,3,2,1,0:T(8,128)(2,1)}, u32[]{:S(2)}, u32[]{:S(2)}) async-start(bf16[8,1,4,128,1024]{4,3,2,1,0:T(8,128)(2,1)} %stack.3), calls=%async_computation.2 | async-start | bytes 16777216 | tf_op jit(solution)/shard_map/all_to_all | solution.py:83
Sparse Core Ops, SparseCore 0:
  191.5 43.6 all-gather.5
  236.9 31.5 all-gather.3
  270.9 71.2 all-reduce.6
  720.0 45.8 all-reduce.4
